TPU v7x, 32 devices: a whole 2x2x4 slice. The times are simulated.
32 devices in a mesh: groups: 2 (over x), gx: 16 (over z, y, core).
Axes of the slice: x: 2, y: 2, z: 4, core: 2. Of those that a mesh axis runs over, the one named last changes fastest.
Arguments:
- features: bfloat16 [64, 16, 64, 128], P(('groups', 'gx')), parts along dimension 0, may hold values from -6 to 6
- cotangent: bfloat16 [64, 16, 64, 128], P(('groups', 'gx')), parts along dimension 0, may hold values from -6 to 6
- wall_flags: int32 [64, 16, 128], P(('groups', 'gx')), parts along dimension 0, may hold values 0 or 1
- mode_counts: int32 [64], replicated, may hold values from 1 to 16, as said below
- offsets: int32 [6, 3], replicated, may hold values from -2 to 2, as said below
- point_weight: bfloat16 [64, 64], replicated, may hold values from -0.75 to 0.75
- kernel_weight: bfloat16 [6, 64, 64], replicated, may hold values from -0.3125 to 0.3125
- lap_weight: bfloat16 [64, 64], replicated, may hold values from -0.125 to 0.125
- spec_weight: bfloat16 [16, 64, 64], replicated, may hold values from -1 to 1
- bias: float32 [64], replicated, may hold values from -3 to 3
Outputs:
- input_grad: bfloat16 [64, 16, 64, 128], P(('groups', 'gx')), parts along dimension 0
- kernel_grad: float32 [12, 64, 64], P('groups'), parts along dimension 0
There are 2 independent parts, one for each index of `groups`. A program takes and returns all parts, laid end to end along the dimension named above; an argument that names none is the same for every part. Nothing has to cross between parts.
Inputs may be any that keep to these rules, and one draw needn't show every extreme that they name: Column 0 holds x offsets in -1..1 and both -1 and 1 occur; columns 1 and 2 hold y and z offsets in -2..2, and -2 and 2 occur in each of them. `mode_counts`: some channel keeps 16 modes and some channel keeps 1.
All inputs are finite; a program needn't handle non-finite values. No bound on the sum of `wall_flags` on one device may be relied on, other than what follows from the above.
Results may differ from a plain program's by a relative error of at most 0.0066.
Values may be sent and summed in bfloat16 or wider, within the bound.
A program may use at most 256 MiB of HBM per device.

v0:
```python
from functools import partial
import math
import jax
import jax.numpy as jnp
from jax import lax
from jax.sharding import PartitionSpec as P

RAD = 2


def with_halo(cells, sides, width):
    for axis, dim in sides:
        count = lax.axis_size(axis)
        ends = count - 1
        head = lax.slice_in_dim(cells, 0, width, axis=dim)
        tail = lax.slice_in_dim(cells, cells.shape[dim] - width, cells.shape[dim], axis=dim)
        cells = jnp.concatenate(
            [
                lax.ppermute(tail, axis, [(i, (i + 1) % count) for i in range(ends)]),
                cells,
                lax.ppermute(head, axis, [((i + 1) % count, i) for i in range(ends)]),
            ],
            axis=dim,
        )
    return cells


def basis_table(mode_total, length):
    mode_index = jnp.arange(mode_total, dtype=jnp.float32)[:, None]
    cell_index = jnp.arange(length, dtype=jnp.float32)[None, :]
    phase_angle = math.pi / (2.0 * length) * mode_index * (2.0 * cell_index + 1.0)
    amplitude = jnp.where(mode_index == 0.0, math.sqrt(1.0 / length), math.sqrt(2.0 / length))
    return (amplitude * jnp.cos(phase_angle)).astype(jnp.bfloat16)


def pencil_work(pencil, spec_weight, kept_modes, adjoint):
    basis = basis_table(spec_weight.shape[0], pencil.shape[0])
    coefficients = jnp.einsum(
        "kx,xycz->kycz", basis, pencil, preferred_element_type=jnp.float32
    ).astype(jnp.bfloat16)
    if adjoint:
        masked = coefficients * kept_modes[:, None, :, None].astype(jnp.bfloat16)
        mixed_modes = jnp.einsum(
            "koc,kyoz->kycz", spec_weight, masked, preferred_element_type=jnp.float32
        ).astype(jnp.bfloat16)
    else:
        mixed_modes = jnp.einsum(
            "koc,kycz->kyoz", spec_weight, coefficients, preferred_element_type=jnp.float32
        )
        mixed_modes = (mixed_modes * kept_modes[:, None, :, None]).astype(jnp.bfloat16)
    return jnp.einsum(
        "kx,kyoz->xyoz", basis, mixed_modes, preferred_element_type=jnp.float32
    ).astype(jnp.bfloat16)


def spectral(slab, spec_weight, kept_modes, adjoint):
    result = pencil_work(
        lax.all_to_all(slab, "gx", split_axis=1, concat_axis=0, tiled=True),
        spec_weight,
        kept_modes,
        adjoint,
    )
    return lax.all_to_all(result, "gx", split_axis=0, concat_axis=1, tiled=True)


def laplace_ext(extended):
    padded = jnp.pad(extended, ((0, 0), (1, 1), (0, 0), (1, 1))).astype(jnp.float32)
    centre_cells = padded[1:-1, 1:-1, :, 1:-1]
    neighbours = padded[2:, 1:-1, :, 1:-1] + padded[:-2, 1:-1, :, 1:-1]
    neighbours = neighbours + padded[1:-1, 2:, :, 1:-1] + padded[1:-1, :-2, :, 1:-1]
    neighbours = neighbours + padded[1:-1, 1:-1, :, 2:] + padded[1:-1, 1:-1, :, :-2]
    return (neighbours - 6.0 * centre_cells).astype(jnp.bfloat16)


def pad_sides(extended):
    return jnp.pad(extended, ((0, 0), (RAD, RAD), (0, 0), (RAD, RAD)))


def window_of(padded, offset, direction, slab_shape):
    starts = (
        1 + direction * offset[0],
        RAD + direction * offset[1],
        0,
        RAD + direction * offset[2],
    )
    return lax.dynamic_slice(padded, starts, slab_shape)


def gelu_slope(preact, upstream):
    _, pullback = jax.vjp(partial(jax.nn.gelu, approximate=True), preact)
    return pullback(upstream)[0]


def per_device(
    features,
    cotangent,
    wall_flags,
    mode_counts,
    offsets,
    point_weight,
    kernel_weight,
    lap_weight,
    spec_weight,
    bias,
):
    mode_total = spec_weight.shape[0]
    tile_total = kernel_weight.shape[0]
    kept_modes = (jnp.arange(mode_total, dtype=jnp.int32)[:, None] < mode_counts[None, :]).astype(
        jnp.float32
    )
    fluid_mask = (1 - wall_flags).astype(jnp.float32)[:, :, None, :]
    extended = with_halo(features, (("gx", 0),), 1)
    padded_field = pad_sides(extended)
    local_part = jnp.einsum(
        "oc,xycz->xyoz", point_weight, features, preferred_element_type=jnp.float32
    )
    local_part = local_part + jnp.einsum(
        "oc,xycz->xyoz", lap_weight, laplace_ext(extended), preferred_element_type=jnp.float32
    )
    for tile in range(tile_total):
        moved = window_of(padded_field, offsets[tile], 1, features.shape)
        local_part = local_part + jnp.einsum(
            "oc,xycz->xyoz", kernel_weight[tile], moved, preferred_element_type=jnp.float32
        )
    local_part = local_part + bias[:, None]
    spectral_part = spectral(features, spec_weight, kept_modes, False)
    preact = local_part + spectral_part.astype(jnp.float32)
    weighted = (gelu_slope(preact, cotangent.astype(jnp.float32)) * fluid_mask).astype(jnp.bfloat16)
    spec_grad = spectral(weighted, spec_weight, kept_modes, True)
    ext_grad = with_halo(weighted, (("gx", 0),), 1)
    padded_grad = pad_sides(ext_grad)
    input_grad = jnp.einsum(
        "oc,xyoz->xycz", point_weight, weighted, preferred_element_type=jnp.float32
    )
    input_grad = input_grad + jnp.einsum(
        "oc,xyoz->xycz", lap_weight, laplace_ext(ext_grad), preferred_element_type=jnp.float32
    )
    input_grad = input_grad + spec_grad.astype(jnp.float32)
    tile_grads = []
    for tile in range(tile_total):
        back_moved = window_of(padded_grad, offsets[tile], -1, weighted.shape)
        input_grad = input_grad + jnp.einsum(
            "oc,xyoz->xycz", kernel_weight[tile], back_moved, preferred_element_type=jnp.float32
        )
        tile_grads.append(
            jnp.einsum("xyoz,xycz->oc", back_moved, features, preferred_element_type=jnp.float32)
        )
    local_grad = jnp.stack(tile_grads, axis=0)
    scaling = float(
        lax.axis_size("gx") * features.shape[0] * features.shape[1] * features.shape[3]
    ) ** (-0.5)
    summed = lax.psum(local_grad, "gx")
    return (input_grad.astype(jnp.bfloat16), summed * scaling)


def solution(mesh):
    return jax.shard_map(
        per_device,
        mesh=mesh,
        in_specs=(
            P(("groups", "gx"), None, None, None),
            P(("groups", "gx"), None, None, None),
            P(("groups", "gx"), None, None),
            P(),
            P(),
            P(),
            P(),
            P(),
            P(),
            P(),
        ),
        out_specs=(P(("groups", "gx"), None, None, None), P("groups", None, None)),
        check_vma=False,
    )
```

profile of v0, /device:TPU:0, one launch (start us, length us, event | category | flops | bytes accessed | tf_op | source)
XLA Modules:
  0.0 241.2 jit_solution(13705008029308537028)
XLA Ops:
  7.2 1.1 fusion.148
  8.4 2.4 collective-permute-start
  10.7 1.3 collective-permute-start.1
  12.0 1.9 copy.40
  13.9 9.4 %all-to-all-start = ((bf16[2,16,64,128]{3,2,0,1:T(8,128)(2,1)}), bf16[2,16,64,128]{3,2,0,1:T(8,128)(2,1)S(1)}, u32[]{:S(2)}, u32[]{:S(2)}) async-start(bf16[2,16,64,128]{3,2,0,1:T(8,128)(2,1)} %copy.40), calls=%async_computation | async-start | bytes 1048576 | tf_op jit(solution)/shard_map/all_to_all | solution.py:58
  23.4 1.3 fusion.76
  61.1 1.5 fusion.48
  62.6 1.4 fusion.49
  64.0 1.1 convolution_convert_fusion.4
  65.3 1.1 fusion.17
  67.4 6.0 %all-to-all-start.1 = ((bf16[32,1,64,128]{3,2,1,0:T(8,128)(2,1)}), bf16[32,1,64,128]{3,2,1,0:T(8,128)(2,1)S(1)}, u32[]{:S(2)}, u32[]{:S(2)}) async-start(bf16[32,1,64,128]{3,2,1,0:T(8,128)(2,1)} %copy.44), calls=%async_computation.1 | async-start | bytes 1048576 | tf_op jit(solution)/shard_map/all_to_all | solution.py:63
  74.2 1.4 fusion.50
  75.7 1.4 fusion.51
  77.1 2.9 %convolution_add_fusion.1 = f32[2,16,128,64]{2,3,1,0:T(8,128)} fusion(f32[2,16,128,64]{2,3,1,0:T(8,128)S(1)} %copy-done.3, f32[4,18,64,130]{3,2,1,0:T(8,128)S(1)} %pad_convert_fusion.1, bf16[64,64]{1,0:T(8,128)(2,1)S(1)} %copy-done.12), kind=kOutput, calls=%fused_computation.37 | convolution fusion | flops 35913728 | bytes 9453568 | tf_op jit(solution)/shard_map/oc,xycz->xyoz/dot_general | solution.py:117
  79.9 8.0 %all-to-all-done.1 = bf16[32,1,64,128]{3,2,1,0:T(8,128)(2,1)S(1)} async-done(((bf16[32,1,64,128]{3,2,1,0:T(8,128)(2,1)}), bf16[32,1,64,128]{3,2,1,0:T(8,128)(2,1)S(1)}, u32[]{:S(2)}, u32[]{:S(2)}) %all-to-all-start.1) | async-done | bytes 524320 | tf_op jit(solution)/shard_map/all_to_all | solution.py:63
  88.7 4.2 %fusion.33 = bf16[2,16,64,128]{3,2,1,0:T(8,128)(2,1)S(1)} fusion(bf16[2,16,64,128]{3,2,1,0:T(8,128)(2,1)} %param.11, f32[2,16,128,64]{2,3,1,0:T(8,128)} %fusion.51, f32[2,16,128,64]{2,3,1,0:T(8,128)} %fusion.50, f32[2,16,128,64]{2,3,1,0:T(8,128)} %fusion.49, f32[2,16,128,64]{2,3,1,0:T(8,128)} %fusion.48, f32[2,16,128,64]{2,3,1,0:T(8,128)S(1)} %fusion.47, ...), kind=kOutput, calls=%fused_computation.72 | convolution fusion | flops 41680896 | bytes 8946188 | tf_op jit(solution)/shard_map/oc,xycz->xyoz/dot_general | solution.py:122
  93.7 1.9 collective-permute-start.2
  95.7 1.3 collective-permute-start.3
  97.0 6.9 %all-to-all-start.2 = ((bf16[2,16,64,128]{3,2,0,1:T(8,128)(2,1)}), bf16[2,16,64,128]{3,2,0,1:T(8,128)(2,1)}, u32[]{:S(2)}, u32[]{:S(2)}) async-start(bf16[2,16,64,128]{3,2,0,1:T(8,128)(2,1)} %copy.49), calls=%async_computation.2 | async-start | bytes 1048576 | tf_op jit(solution)/shard_map/all_to_all | solution.py:58
  103.9 1.3 fusion.74
  110.9 1.5 convolution_bitcast_fusion.2
  112.3 1.4 convolution_bitcast_fusion.3
  113.7 4.7 %all-to-all-done.2 = bf16[2,16,64,128]{3,2,0,1:T(8,128)(2,1)} async-done(((bf16[2,16,64,128]{3,2,0,1:T(8,128)(2,1)}), bf16[2,16,64,128]{3,2,0,1:T(8,128)(2,1)}, u32[]{:S(2)}, u32[]{:S(2)}) %all-to-all-start.2) | async-done | bytes 524320 | tf_op jit(solution)/shard_map/all_to_all | solution.py:58
  118.4 1.5 fusion.22
  121.7 4.1 %all-to-all-start.3 = ((bf16[32,1,64,128]{3,2,1,0:T(8,128)(2,1)}), bf16[32,1,64,128]{3,2,1,0:T(8,128)(2,1)S(1)}, u32[]{:S(2)}, u32[]{:S(2)}) async-start(bf16[32,1,64,128]{3,2,1,0:T(8,128)(2,1)} %copy.55), calls=%async_computation.3 | async-start | bytes 1048576 | tf_op jit(solution)/shard_map/all_to_all | solution.py:63
  126.9 1.4 convolution_bitcast_fusion.4
  128.3 1.5 convolution_bitcast_fusion
  129.8 2.9 %pad_convert_fusion = f32[4,18,64,130]{3,2,1,0:T(8,128)} fusion(bf16[4,16,64,128]{3,2,1,0:T(8,128)(2,1)S(1)} %pad_maximum_fusion), kind=kLoop, calls=%fused_computation.12 | loop fusion | flops 599040 | bytes 3444736 | tf_op jit(solution)/shard_map/convert_element_type | solution.py:67
  132.7 89.0 %all-reduce.6.cloned.1.call-done = f32[6,64,64]{2,1,0:T(8,128)} async-done(((f32[6,64,64]{2,1,0:T(8,128)}), f32[6,64,64]{2,1,0:T(8,128)}) %all-reduce.6.cloned.1.call-update) | async-done | bytes 98320 | tf_op jit(solution)/shard_map/psum | solution.py:152
  221.7 1.6 broadcast_multiply_fusion
  223.4 7.5 %fusion.15 = f32[2,16,64,128]{3,2,1,0:T(8,128)S(1)} fusion(f32[2,16,128,64]{2,3,1,0:T(8,128)} %fusion.74, f32[4,18,64,130]{3,2,1,0:T(8,128)} %pad_convert_fusion, bf16[64,64]{1,0:T(8,128)(2,1)S(1)} %copy-done.13, bf16[16,2,1,64,128]{4,3,1,0,2:T(8,128)(2,1)S(1)} %bitcast.306), kind=kOutput, calls=%fused_computation.40 | convolution fusion | flops 36438016 | bytes 9969664 | tf_op jit(solution)/shard_map/oc,xyoz->xycz/dot_general | solution.py:135
  230.8 3.5 %fusion.16 = bf16[2,16,64,128]{3,2,1,0:T(8,128)(2,1)} fusion(f32[2,16,64,128]{3,2,1,0:T(8,128)} %convolution_bitcast_fusion, f32[2,16,64,128]{3,2,1,0:T(8,128)S(1)} %convolution_bitcast_fusion.1, f32[2,16,64,128]{3,2,1,0:T(8,128)} %convolution_bitcast_fusion.2, f32[2,16,64,128]{3,2,1,0:T(8,128)} %convolution_bitcast_fusion.3, ...), kind=kOutput, calls=%fused_computation.43 | convolution fusion | flops 35389440 | bytes 7880716 | tf_op jit(solution)/shard_map/oc,xyoz->xycz/dot_general | solution.py:142
  (62 shorter events, 14.6 us)
Async XLA Ops:
  7.2 57.9 %copy-start = (bf16[16,64,64]{2,1,0:T(8,128)(2,1)S(1)}, bf16[16,64,64]{2,1,0:T(8,128)(2,1)}, u32[]{:S(2)}) copy-start(bf16[16,64,64]{2,1,0:T(8,128)(2,1)} %param.18) | copy-start | bytes 393220
  7.2 16.2 %copy-start.1 = (bf16[2,16,64,128]{3,2,1,0:T(8,128)(2,1)S(1)}, bf16[2,16,64,128]{3,2,1,0:T(8,128)(2,1)}, u32[]{:S(2)}) copy-start(bf16[2,16,64,128]{3,2,1,0:T(8,128)(2,1)} %param.10) | copy-start | bytes 1572868
  7.2 16.2 %copy-start.11 = (s32[64]{0:T(128)S(1)}, s32[64]{0:T(128)}, u32[]{:S(2)}) copy-start(s32[64]{0:T(128)} %param.13) | copy-start | bytes 772
  7.2 16.2 %copy-start.5 = (bf16[64,64]{1,0:T(8,128)(2,1)S(1)}, bf16[64,64]{1,0:T(8,128)(2,1)}, u32[]{:S(2)}) copy-start(bf16[64,64]{1,0:T(8,128)(2,1)} %param.15) | copy-start | bytes 24580
  7.2 17.5 %copy-start.8 = (s32[2,16,128]{2,1,0:T(8,128)S(1)}, s32[2,16,128]{2,1,0:T(8,128)}, u32[]{:S(2)}) copy-start(s32[2,16,128]{2,1,0:T(8,128)} %param.12) | copy-start | bytes 49156
  7.2 17.5 %copy-start.6 = (s32[6,3]{0,1:T(4,128)S(1)}, s32[6,3]{0,1:T(4,128)}, u32[]{:S(2)}) copy-start(s32[6,3]{0,1:T(4,128)} %param.14) | copy-start | bytes 220
  8.4 52.2 %collective-permute-start = (bf16[1,16,64,128]{3,2,1,0:T(8,128)(2,1)S(1)}, bf16[1,16,64,128]{3,2,1,0:T(8,128)(2,1)S(1)}, u32[]{:S(2)}, u32[]{:S(2)}) collective-permute-start(bf16[1,16,64,128]{3,2,1,0:T(8,128)(2,1)S(1)} %get-tuple-element.5), channel_id=1, source_target_pairs={{0,1},{1,2},{2,3},{3,4},{4,5},{5,6},{6,7},{7,8},{8,9},{9,10},{10,1... | collective-permute-start | bytes 786440 | tf_op jit(solution)/shard_map/ppermute | solution.py:19
  10.7 49.9 %collective-permute-start.1 = (bf16[1,16,64,128]{3,2,1,0:T(8,128)(2,1)S(1)}, bf16[1,16,64,128]{3,2,1,0:T(8,128)(2,1)S(1)}, u32[]{:S(2)}, u32[]{:S(2)}) collective-permute-start(bf16[1,16,64,128]{3,2,1,0:T(8,128)(2,1)S(1)} %get-tuple-element.4), channel_id=1, source_target_pairs={{1,0},{2,1},{3,2},{4,3},{5,4},{6,5},{7,6},{8,7},{9,8},{10,9},{11,1... | collective-permute-start | bytes 786440 | tf_op jit(solution)/shard_map/ppermute | solution.py:21
  13.9 46.8 %copy-start.4 = (bf16[6,64,64]{2,1,0:T(8,128)(2,1)S(1)}, bf16[6,64,64]{2,1,0:T(8,128)(2,1)}, u32[]{:S(2)}) copy-start(bf16[6,64,64]{2,1,0:T(8,128)(2,1)} %param.16) | copy-start | bytes 147460
  13.9 50.1 %all-to-all-start = ((bf16[2,16,64,128]{3,2,0,1:T(8,128)(2,1)}), bf16[2,16,64,128]{3,2,0,1:T(8,128)(2,1)S(1)}, u32[]{:S(2)}, u32[]{:S(2)}) async-start(bf16[2,16,64,128]{3,2,0,1:T(8,128)(2,1)} %copy.40), calls=%async_computation | async-start | bytes 1048576 | tf_op jit(solution)/shard_map/all_to_all | solution.py:58
  67.4 20.5 %all-to-all-start.1 = ((bf16[32,1,64,128]{3,2,1,0:T(8,128)(2,1)}), bf16[32,1,64,128]{3,2,1,0:T(8,128)(2,1)S(1)}, u32[]{:S(2)}, u32[]{:S(2)}) async-start(bf16[32,1,64,128]{3,2,1,0:T(8,128)(2,1)} %copy.44), calls=%async_computation.1 | async-start | bytes 1048576 | tf_op jit(solution)/shard_map/all_to_all | solution.py:63
  74.2 2.9 %copy-start.3 = (f32[2,16,128,64]{2,3,1,0:T(8,128)S(1)}, f32[2,16,128,64]{2,3,1,0:T(8,128)}, u32[]{:S(2)}) copy-start(f32[2,16,128,64]{2,3,1,0:T(8,128)} %fusion.76) | copy-start | bytes 3145732
  74.2 2.9 %copy-start.12 = (bf16[64,64]{1,0:T(8,128)(2,1)S(1)}, bf16[64,64]{1,0:T(8,128)(2,1)}, u32[]{:S(2)}) copy-start(bf16[64,64]{1,0:T(8,128)(2,1)} %param.17) | copy-start | bytes 24580
  75.7 13.0 %copy-start.10 = (f32[64]{0:T(128)S(1)}, f32[64]{0:T(128)}, u32[]{:S(2)}) copy-start(f32[64]{0:T(128)} %param.19) | copy-start | bytes 772
  87.9 0.8 copy-start.2
  93.7 11.5 %collective-permute-start.2 = (bf16[1,16,64,128]{3,2,1,0:T(8,128)(2,1)S(1)}, bf16[1,16,64,128]{3,2,1,0:T(8,128)(2,1)S(1)}, u32[]{:S(2)}, u32[]{:S(2)}) collective-permute-start(bf16[1,16,64,128]{3,2,1,0:T(8,128)(2,1)S(1)} %get-tuple-element.2), channel_id=1, source_target_pairs={{0,1},{1,2},{2,3},{3,4},{4,5},{5,6},{6,7},{7,8},{8,9},{9,10},{10,1... | collective-permute-start | bytes 786440 | tf_op jit(solution)/shard_map/ppermute | solution.py:19
  95.7 9.6 %collective-permute-start.3 = (bf16[1,16,64,128]{3,2,1,0:T(8,128)(2,1)S(1)}, bf16[1,16,64,128]{3,2,1,0:T(8,128)(2,1)S(1)}, u32[]{:S(2)}, u32[]{:S(2)}) collective-permute-start(bf16[1,16,64,128]{3,2,1,0:T(8,128)(2,1)S(1)} %get-tuple-element.3), channel_id=1, source_target_pairs={{1,0},{2,1},{3,2},{4,3},{5,4},{6,5},{7,6},{8,7},{9,8},{10,9},{11,1... | collective-permute-start | bytes 786440 | tf_op jit(solution)/shard_map/ppermute | solution.py:21
  97.0 21.5 %all-to-all-start.2 = ((bf16[2,16,64,128]{3,2,0,1:T(8,128)(2,1)}), bf16[2,16,64,128]{3,2,0,1:T(8,128)(2,1)}, u32[]{:S(2)}, u32[]{:S(2)}) async-start(bf16[2,16,64,128]{3,2,0,1:T(8,128)(2,1)} %copy.49), calls=%async_computation.2 | async-start | bytes 1048576 | tf_op jit(solution)/shard_map/all_to_all | solution.py:58
  110.8 7.6 %copy-start.7 = (bf16[16,64]{0,1:T(8,128)(2,1)S(1)}, bf16[16,64]{0,1:T(8,128)(2,1)}, u32[]{:S(2)}) copy-start(bf16[16,64]{0,1:T(8,128)(2,1)} %copy.51) | copy-start | bytes 6148
  110.8 7.6 %copy-start.9 = (f32[32]{0:T(128)S(1)}, f32[32]{0:T(128)}, u32[]{:S(2)}) copy-start(f32[32]{0:T(128)} %multiply_add_fusion) | copy-start | bytes 388
  121.7 101.7 %all-to-all-start.3 = ((bf16[32,1,64,128]{3,2,1,0:T(8,128)(2,1)}), bf16[32,1,64,128]{3,2,1,0:T(8,128)(2,1)S(1)}, u32[]{:S(2)}, u32[]{:S(2)}) async-start(bf16[32,1,64,128]{3,2,1,0:T(8,128)(2,1)} %copy.55), calls=%async_computation.3 | async-start | bytes 1048576 | tf_op jit(solution)/shard_map/all_to_all | solution.py:63
  125.8 95.9 %all-reduce.6.cloned.1.call-start = ((), (), s32[]{:S(2)}) async-start(), calls=%async_computation.4 | async-start | bytes 393216 | tf_op jit(solution)/shard_map/psum | solution.py:152
  129.8 93.6 %copy-start.13 = (bf16[64,64]{1,0:T(8,128)(2,1)S(1)}, bf16[64,64]{1,0:T(8,128)(2,1)}, u32[]{:S(2)}) copy-start(bf16[64,64]{1,0:T(8,128)(2,1)} %param.17) | copy-start | bytes 24580
Sparse Core Ops, SparseCore 0:
  130.6 91.0 all-reduce.5
where the time goes:
time: 242 us; the launch traced here: 241 us
  waiting for transfers between devices  102 us (42%)
  between operations  48.2 us (20%)
  matrix products  43.7 us (18%)
  starting transfers between devices  33.4 us (14%)
  local copies, waits for them, and re-layouts  8.26 us (3%)
  other arithmetic  5.98 us (2%)
    psum x1, waiting for transfers between devices, per_device(): summed = lax.psum(local_grad, 'gx')  89 us
    all_to_all x2, starting transfers between devices, spectral(): lax.all_to_all(slab, 'gx', split_axis=1, concat_axis=0, tiled=True)  16.4 us
    dot_general x6, matrix products, per_device(): jnp.einsum('oc,xycz->xyoz', kernel_weight[tile], moved, preferred_element...  10.4 us
    all_to_all x2, starting transfers between devices, spectral(): return lax.all_to_all(result, 'gx', split_axis=0, concat_axis=1, tiled=True)  10.1 us
    dot_general x6, matrix products, per_device(): jnp.einsum('oc,xyoz->xycz', kernel_weight[tile], back_moved, preferred_el...  9.73 us
    all_to_all x2, waiting for transfers between devices, spectral(): return lax.all_to_all(result, 'gx', split_axis=0, concat_axis=1, tiled=True)  7.95 us
    dot_general x1, matrix products, per_device(): jnp.einsum('oc,xyoz->xycz', lap_weight, laplace_ext(ext_grad), preferred_...  7.47 us
    dot_general x6, matrix products, per_device(): jnp.einsum('xyoz,xycz->oc', back_moved, features, preferred_element_type=...  6.05 us
  transfers between devices with their start and end apart: 9, of which 3 were waited for; matrix products, arithmetic and copies ran while one was open for 14% of the time, Pallas kernels for 0%

commit v1 on v0

--- a/solution.py
+++ b/solution.py
@@ -149,7 +149,8 @@
     scaling = float(
         lax.axis_size("gx") * features.shape[0] * features.shape[1] * features.shape[3]
     ) ** (-0.5)
-    summed = lax.psum(local_grad, "gx")
+    pieces = lax.all_gather(local_grad, "gx")
+    summed = jnp.sum(pieces, axis=0)
     return (input_grad.astype(jnp.bfloat16), summed * scaling)
 
 

time: 242 us -> 167 us (0.69)
  waiting for transfers between devices: 102 us -> 30 us
  matrix products: 43.7 us -> 37.8 us
    psum x1 -> x0, waiting for transfers between devices: 89 us -> none  [per_device(): summed = lax.psum(local_grad, 'gx')]
    all_to_all x2, waiting for transfers between devices: 7.95 us -> 15.4 us  [spectral(): return lax.all_to_all(result, 'gx', split_axis=0, concat_axis=1, tiled=True)]
    all_gather x0 -> x1, waiting for transfers between devices: none -> 6.79 us  [per_device(): pieces = lax.all_gather(local_grad, 'gx')]
    dot_general x6, matrix products: 6.05 us -> 2.36 us  [per_device(): jnp.einsum('xyoz,xycz->oc', back_moved, features, preferred_element_type=...]
    all_to_all x2, waiting for transfers between devices: 4.71 us -> 7.82 us  [spectral(): lax.all_to_all(slab, 'gx', split_axis=1, concat_axis=0, tiled=True)]
  transfers between devices with their start and end apart: 9 -> 9, of which waited for: 3 -> 4; matrix products, arithmetic and copies ran while one was open for 14% -> 25% of each run, Pallas kernels for 0% -> 0%
where the time goes in v1:
time: 167 us; the launch traced here: 166 us
  between operations  48.6 us (29%)
  matrix products  37.8 us (23%)
  starting transfers between devices  33.6 us (20%)
  waiting for transfers between devices  30 us (18%)
  local copies, waits for them, and re-layouts  8.37 us (5%)
  other arithmetic  7.79 us (5%)
    all_to_all x2, starting transfers between devices, spectral(): lax.all_to_all(slab, 'gx', split_axis=1, concat_axis=0, tiled=True)  16.3 us
    all_to_all x2, waiting for transfers between devices, spectral(): return lax.all_to_all(result, 'gx', split_axis=0, concat_axis=1, tiled=True)  15.4 us
    dot_general x6, matrix products, per_device(): jnp.einsum('oc,xycz->xyoz', kernel_weight[tile], moved, preferred_element...  10.4 us
    all_to_all x2, starting transfers between devices, spectral(): return lax.all_to_all(result, 'gx', split_axis=0, concat_axis=1, tiled=True)  10.1 us
    all_to_all x2, waiting for transfers between devices, spectral(): lax.all_to_all(slab, 'gx', split_axis=1, concat_axis=0, tiled=True)  7.82 us
    dot_general x1, matrix products, per_device(): jnp.einsum('oc,xyoz->xycz', lap_weight, laplace_ext(ext_grad), preferred_...  7.58 us
    dot_general x6, matrix products, per_device(): jnp.einsum('oc,xyoz->xycz', kernel_weight[tile], back_moved, preferred_el...  7.52 us
    all_gather x1, waiting for transfers between devices, per_device(): pieces = lax.all_gather(local_grad, 'gx')  6.79 us
  transfers between devices with their start and end apart: 9, of which 4 were waited for; matrix products, arithmetic and copies ran while one was open for 25% of the time, Pallas kernels for 0%

profile of v1, /device:TPU:0, one launch (start us, length us, event | category | flops | bytes accessed | tf_op | source)
XLA Modules:
  0.0 166.1 jit_solution(18212611988768496173)
XLA Ops:
  7.2 1.1 fusion.148
  8.4 2.4 %collective-permute-start = (bf16[1,16,64,128]{3,2,1,0:T(8,128)(2,1)S(1)}, bf16[1,16,64,128]{3,2,1,0:T(8,128)(2,1)S(1)}, u32[]{:S(2)}, u32[]{:S(2)}) collective-permute-start(bf16[1,16,64,128]{3,2,1,0:T(8,128)(2,1)S(1)} %get-tuple-element.5), channel_id=1, source_target_pairs={{0,1},{1,2},{2,3},{3,4},{4,5},{5,6},{6,7},{7,8},{8,9},{9,10},{10,1... | collective-permute-start | bytes 786440 | tf_op jit(solution)/shard_map/ppermute | solution.py:19
  10.7 1.3 collective-permute-start.1
  12.0 1.9 %copy.40 = bf16[2,16,64,128]{3,2,0,1:T(8,128)(2,1)} copy(bf16[2,16,64,128]{3,2,1,0:T(8,128)(2,1)} %param.10) | data formatting | bytes 1048576 | tf_op args[0]
  13.9 9.4 %all-to-all-start = ((bf16[2,16,64,128]{3,2,0,1:T(8,128)(2,1)}), bf16[2,16,64,128]{3,2,0,1:T(8,128)(2,1)S(1)}, u32[]{:S(2)}, u32[]{:S(2)}) async-start(bf16[2,16,64,128]{3,2,0,1:T(8,128)(2,1)} %copy.40), calls=%async_computation | async-start | bytes 1048576 | tf_op jit(solution)/shard_map/all_to_all | solution.py:58
  23.4 1.3 fusion.76
  49.7 1.5 fusion.48
  51.2 1.4 fusion.49
  52.6 1.1 convolution_convert_fusion.4
  56.0 6.0 %all-to-all-start.1 = ((bf16[32,1,64,128]{3,2,1,0:T(8,128)(2,1)}), bf16[32,1,64,128]{3,2,1,0:T(8,128)(2,1)S(1)}, u32[]{:S(2)}, u32[]{:S(2)}) async-start(bf16[32,1,64,128]{3,2,1,0:T(8,128)(2,1)} %copy.44), calls=%async_computation.1 | async-start | bytes 1048576 | tf_op jit(solution)/shard_map/all_to_all | solution.py:63
  62.8 1.4 fusion.50
  64.2 1.4 fusion.51
  65.6 2.8 %convolution_add_fusion.1 = f32[2,16,128,64]{2,3,1,0:T(8,128)} fusion(f32[2,16,128,64]{2,3,1,0:T(8,128)S(1)} %copy-done.7, f32[4,18,64,130]{3,2,1,0:T(8,128)S(1)} %pad_convert_fusion.1, bf16[64,64]{1,0:T(8,128)(2,1)S(1)} %copy-done.17), kind=kOutput, calls=%fused_computation.37 | convolution fusion | flops 35913728 | bytes 9453568 | tf_op jit(solution)/shard_map/oc,xycz->xyoz/dot_general | solution.py:117
  68.5 8.0 %all-to-all-done.1 = bf16[32,1,64,128]{3,2,1,0:T(8,128)(2,1)S(1)} async-done(((bf16[32,1,64,128]{3,2,1,0:T(8,128)(2,1)}), bf16[32,1,64,128]{3,2,1,0:T(8,128)(2,1)S(1)}, u32[]{:S(2)}, u32[]{:S(2)}) %all-to-all-start.1) | async-done | bytes 524320 | tf_op jit(solution)/shard_map/all_to_all | solution.py:63
  77.2 4.2 %fusion.33 = bf16[2,16,64,128]{3,2,1,0:T(8,128)(2,1)S(1)} fusion(bf16[2,16,64,128]{3,2,1,0:T(8,128)(2,1)} %param.11, f32[2,16,128,64]{2,3,1,0:T(8,128)} %fusion.51, f32[2,16,128,64]{2,3,1,0:T(8,128)} %fusion.50, f32[2,16,128,64]{2,3,1,0:T(8,128)} %fusion.49, f32[2,16,128,64]{2,3,1,0:T(8,128)} %fusion.48, f32[2,16,128,64]{2,3,1,0:T(8,128)S(1)} %fusion.47, ...), kind=kOutput, calls=%fused_computation.72 | convolution fusion | flops 41680896 | bytes 8946188 | tf_op jit(solution)/shard_map/oc,xycz->xyoz/dot_general | solution.py:122
  81.5 1.9 %collective-permute-start.2 = (bf16[1,16,64,128]{3,2,1,0:T(8,128)(2,1)S(1)}, bf16[1,16,64,128]{3,2,1,0:T(8,128)(2,1)S(1)}, u32[]{:S(2)}, u32[]{:S(2)}) collective-permute-start(bf16[1,16,64,128]{3,2,1,0:T(8,128)(2,1)S(1)} %get-tuple-element.2), channel_id=1, source_target_pairs={{0,1},{1,2},{2,3},{3,4},{4,5},{5,6},{6,7},{7,8},{8,9},{9,10},{10,1... | collective-permute-start | bytes 786440 | tf_op jit(solution)/shard_map/ppermute | solution.py:19
  83.4 1.3 collective-permute-start.3
  97.1 6.9 %all-to-all-start.2 = ((bf16[2,16,64,128]{3,2,0,1:T(8,128)(2,1)}), bf16[2,16,64,128]{3,2,0,1:T(8,128)(2,1)}, u32[]{:S(2)}, u32[]{:S(2)}) async-start(bf16[2,16,64,128]{3,2,0,1:T(8,128)(2,1)} %copy.49), calls=%async_computation.2 | async-start | bytes 1048576 | tf_op jit(solution)/shard_map/all_to_all | solution.py:58
  107.6 1.3 fusion.74
  109.3 1.5 convolution_bitcast_fusion.2
  110.8 7.8 %all-to-all-done.2 = bf16[2,16,64,128]{3,2,0,1:T(8,128)(2,1)} async-done(((bf16[2,16,64,128]{3,2,0,1:T(8,128)(2,1)}), bf16[2,16,64,128]{3,2,0,1:T(8,128)(2,1)}, u32[]{:S(2)}, u32[]{:S(2)}) %all-to-all-start.2) | async-done | bytes 524320 | tf_op jit(solution)/shard_map/all_to_all | solution.py:58
  118.6 1.5 fusion.22
  121.9 4.1 %all-to-all-start.3 = ((bf16[32,1,64,128]{3,2,1,0:T(8,128)(2,1)}), bf16[32,1,64,128]{3,2,1,0:T(8,128)(2,1)S(1)}, u32[]{:S(2)}, u32[]{:S(2)}) async-start(bf16[32,1,64,128]{3,2,1,0:T(8,128)(2,1)} %copy.55), calls=%async_computation.3 | async-start | bytes 1048576 | tf_op jit(solution)/shard_map/all_to_all | solution.py:63
  126.0 2.9 %pad_convert_fusion = f32[4,18,64,130]{3,2,1,0:T(8,128)} fusion(bf16[4,16,64,128]{3,2,1,0:T(8,128)(2,1)S(1)} %pad_maximum_fusion), kind=kLoop, calls=%fused_computation.12 | loop fusion | flops 599040 | bytes 3444736 | tf_op jit(solution)/shard_map/convert_element_type | solution.py:67
  128.9 1.4 convolution_bitcast_fusion.3
  130.3 1.5 convolution_bitcast_fusion.4
  131.7 1.4 convolution_bitcast_fusion
  133.1 7.4 %all-to-all-done.3 = bf16[32,1,64,128]{3,2,1,0:T(8,128)(2,1)S(1)} async-done(((bf16[32,1,64,128]{3,2,1,0:T(8,128)(2,1)}), bf16[32,1,64,128]{3,2,1,0:T(8,128)(2,1)S(1)}, u32[]{:S(2)}, u32[]{:S(2)}) %all-to-all-start.3) | async-done | bytes 524320 | tf_op jit(solution)/shard_map/all_to_all | solution.py:63
  140.6 7.6 %fusion.15 = f32[2,16,64,128]{3,2,1,0:T(8,128)S(1)} fusion(f32[2,16,128,64]{2,3,1,0:T(8,128)} %fusion.74, f32[4,18,64,130]{3,2,1,0:T(8,128)} %pad_convert_fusion, bf16[64,64]{1,0:T(8,128)(2,1)S(1)} %copy-done.18, bf16[16,2,1,64,128]{4,3,1,0,2:T(8,128)(2,1)S(1)} %bitcast.308), kind=kOutput, calls=%fused_computation.40 | convolution fusion | flops 36438016 | bytes 9969664 | tf_op jit(solution)/shard_map/oc,xyoz->xycz/dot_general | solution.py:135
  148.2 1.4 fusion.16
  149.6 6.8 %all-gather.3.cloned.1.call-done = f32[96,64,64]{2,1,0:T(8,128)} async-done(((f32[6,64,64]{2,1,0:T(8,128)}), f32[96,64,64]{2,1,0:T(8,128)}) %all-gather.3.cloned.1.call-update) | async-done | bytes 1572880 | tf_op jit(solution)/shard_map/all_gather | solution.py:152
  156.3 2.3 %reduce_sum.9 = f32[6,64,64]{2,1,0:T(8,128)S(1)} reduce(f32[16,6,64,64]{3,2,1,0:T(8,128)} %bitcast.305, f32[]{:T(128)} %constant.158.clone.1), dimensions={0}, to_apply=%region_0.1 | reduce | flops 368640 | bytes 1671172 | tf_op jit(solution)/shard_map/reduce_sum | solution.py:153
  (73 shorter events, 13.5 us)
Async XLA Ops:
  7.2 46.5 %copy-start = (bf16[16,64,64]{2,1,0:T(8,128)(2,1)S(1)}, bf16[16,64,64]{2,1,0:T(8,128)(2,1)}, u32[]{:S(2)}) copy-start(bf16[16,64,64]{2,1,0:T(8,128)(2,1)} %param.18) | copy-start | bytes 393220
  7.2 16.2 %copy-start.1 = (bf16[2,16,64,128]{3,2,1,0:T(8,128)(2,1)S(1)}, bf16[2,16,64,128]{3,2,1,0:T(8,128)(2,1)}, u32[]{:S(2)}) copy-start(bf16[2,16,64,128]{3,2,1,0:T(8,128)(2,1)} %param.10) | copy-start | bytes 1572868
  7.2 16.2 %copy-start.16 = (s32[64]{0:T(128)S(1)}, s32[64]{0:T(128)}, u32[]{:S(2)}) copy-start(s32[64]{0:T(128)} %param.13) | copy-start | bytes 772
  7.2 16.2 %copy-start.10 = (bf16[64,64]{1,0:T(8,128)(2,1)S(1)}, bf16[64,64]{1,0:T(8,128)(2,1)}, u32[]{:S(2)}) copy-start(bf16[64,64]{1,0:T(8,128)(2,1)} %param.15) | copy-start | bytes 24580
  7.2 17.4 %copy-start.12 = (s32[2,16,128]{2,1,0:T(8,128)S(1)}, s32[2,16,128]{2,1,0:T(8,128)}, u32[]{:S(2)}) copy-start(s32[2,16,128]{2,1,0:T(8,128)} %param.12) | copy-start | bytes 49156
  7.2 18.0 %copy-start.11 = (s32[6,3]{0,1:T(4,128)S(1)}, s32[6,3]{0,1:T(4,128)}, u32[]{:S(2)}) copy-start(s32[6,3]{0,1:T(4,128)} %param.14) | copy-start | bytes 220
  8.4 40.7 %collective-permute-start = (bf16[1,16,64,128]{3,2,1,0:T(8,128)(2,1)S(1)}, bf16[1,16,64,128]{3,2,1,0:T(8,128)(2,1)S(1)}, u32[]{:S(2)}, u32[]{:S(2)}) collective-permute-start(bf16[1,16,64,128]{3,2,1,0:T(8,128)(2,1)S(1)} %get-tuple-element.5), channel_id=1, source_target_pairs={{0,1},{1,2},{2,3},{3,4},{4,5},{5,6},{6,7},{7,8},{8,9},{9,10},{10,1... | collective-permute-start | bytes 786440 | tf_op jit(solution)/shard_map/ppermute | solution.py:19
  10.7 38.4 %collective-permute-start.1 = (bf16[1,16,64,128]{3,2,1,0:T(8,128)(2,1)S(1)}, bf16[1,16,64,128]{3,2,1,0:T(8,128)(2,1)S(1)}, u32[]{:S(2)}, u32[]{:S(2)}) collective-permute-start(bf16[1,16,64,128]{3,2,1,0:T(8,128)(2,1)S(1)} %get-tuple-element.4), channel_id=1, source_target_pairs={{1,0},{2,1},{3,2},{4,3},{5,4},{6,5},{7,6},{8,7},{9,8},{10,9},{11,1... | collective-permute-start | bytes 786440 | tf_op jit(solution)/shard_map/ppermute | solution.py:21
  13.9 35.3 %copy-start.8 = (bf16[6,64,64]{2,1,0:T(8,128)(2,1)S(1)}, bf16[6,64,64]{2,1,0:T(8,128)(2,1)}, u32[]{:S(2)}) copy-start(bf16[6,64,64]{2,1,0:T(8,128)(2,1)} %param.16) | copy-start | bytes 147460
  13.9 38.7 %all-to-all-start = ((bf16[2,16,64,128]{3,2,0,1:T(8,128)(2,1)}), bf16[2,16,64,128]{3,2,0,1:T(8,128)(2,1)S(1)}, u32[]{:S(2)}, u32[]{:S(2)}) async-start(bf16[2,16,64,128]{3,2,0,1:T(8,128)(2,1)} %copy.40), calls=%async_computation | async-start | bytes 1048576 | tf_op jit(solution)/shard_map/all_to_all | solution.py:58
  56.0 20.5 %all-to-all-start.1 = ((bf16[32,1,64,128]{3,2,1,0:T(8,128)(2,1)}), bf16[32,1,64,128]{3,2,1,0:T(8,128)(2,1)S(1)}, u32[]{:S(2)}, u32[]{:S(2)}) async-start(bf16[32,1,64,128]{3,2,1,0:T(8,128)(2,1)} %copy.44), calls=%async_computation.1 | async-start | bytes 1048576 | tf_op jit(solution)/shard_map/all_to_all | solution.py:63
  62.8 2.9 %copy-start.7 = (f32[2,16,128,64]{2,3,1,0:T(8,128)S(1)}, f32[2,16,128,64]{2,3,1,0:T(8,128)}, u32[]{:S(2)}) copy-start(f32[2,16,128,64]{2,3,1,0:T(8,128)} %fusion.76) | copy-start | bytes 3145732
  62.8 2.9 %copy-start.17 = (bf16[64,64]{1,0:T(8,128)(2,1)S(1)}, bf16[64,64]{1,0:T(8,128)(2,1)}, u32[]{:S(2)}) copy-start(bf16[64,64]{1,0:T(8,128)(2,1)} %param.17) | copy-start | bytes 24580
  64.2 13.0 %copy-start.15 = (f32[64]{0:T(128)S(1)}, f32[64]{0:T(128)}, u32[]{:S(2)}) copy-start(f32[64]{0:T(128)} %param.19) | copy-start | bytes 772
  76.4 0.8 copy-start.6
  81.5 22.8 %collective-permute-start.2 = (bf16[1,16,64,128]{3,2,1,0:T(8,128)(2,1)S(1)}, bf16[1,16,64,128]{3,2,1,0:T(8,128)(2,1)S(1)}, u32[]{:S(2)}, u32[]{:S(2)}) collective-permute-start(bf16[1,16,64,128]{3,2,1,0:T(8,128)(2,1)S(1)} %get-tuple-element.2), channel_id=1, source_target_pairs={{0,1},{1,2},{2,3},{3,4},{4,5},{5,6},{6,7},{7,8},{8,9},{9,10},{10,1... | collective-permute-start | bytes 786440 | tf_op jit(solution)/shard_map/ppermute | solution.py:19
  83.4 20.9 %collective-permute-start.3 = (bf16[1,16,64,128]{3,2,1,0:T(8,128)(2,1)S(1)}, bf16[1,16,64,128]{3,2,1,0:T(8,128)(2,1)S(1)}, u32[]{:S(2)}, u32[]{:S(2)}) collective-permute-start(bf16[1,16,64,128]{3,2,1,0:T(8,128)(2,1)S(1)} %get-tuple-element.3), channel_id=1, source_target_pairs={{1,0},{2,1},{3,2},{4,3},{5,4},{6,5},{7,6},{8,7},{9,8},{10,9},{11,1... | collective-permute-start | bytes 786440 | tf_op jit(solution)/shard_map/ppermute | solution.py:21
  97.1 21.5 %all-to-all-start.2 = ((bf16[2,16,64,128]{3,2,0,1:T(8,128)(2,1)}), bf16[2,16,64,128]{3,2,0,1:T(8,128)(2,1)}, u32[]{:S(2)}, u32[]{:S(2)}) async-start(bf16[2,16,64,128]{3,2,0,1:T(8,128)(2,1)} %copy.49), calls=%async_computation.2 | async-start | bytes 1048576 | tf_op jit(solution)/shard_map/all_to_all | solution.py:58
  104.1 52.3 %all-gather.3.cloned.1.call-start = ((), (), s32[]{:S(2)}) async-start(), calls=%async_computation.4 | async-start | bytes 3342336 | tf_op jit(solution)/shard_map/all_gather | solution.py:152
  106.9 0.7 copy-start.9
  107.6 11.0 %copy-start.13 = (f32[16]{0:T(128)S(1)}, f32[16]{0:T(128)}, u32[]{:S(2)}) copy-start(f32[16]{0:T(128)} %get-tuple-element.27) | copy-start | bytes 196
  107.6 11.0 %copy-start.14 = (f32[32]{0:T(128)S(1)}, f32[32]{0:T(128)}, u32[]{:S(2)}) copy-start(f32[32]{0:T(128)} %multiply_add_fusion) | copy-start | bytes 388
  121.9 18.7 %all-to-all-start.3 = ((bf16[32,1,64,128]{3,2,1,0:T(8,128)(2,1)}), bf16[32,1,64,128]{3,2,1,0:T(8,128)(2,1)S(1)}, u32[]{:S(2)}, u32[]{:S(2)}) async-start(bf16[32,1,64,128]{3,2,1,0:T(8,128)(2,1)} %copy.55), calls=%async_computation.3 | async-start | bytes 1048576 | tf_op jit(solution)/shard_map/all_to_all | solution.py:63
  130.3 10.3 %copy-start.18 = (bf16[64,64]{1,0:T(8,128)(2,1)S(1)}, bf16[64,64]{1,0:T(8,128)(2,1)}, u32[]{:S(2)}) copy-start(bf16[64,64]{1,0:T(8,128)(2,1)} %param.17) | copy-start | bytes 24580
  140.5 7.6 %copy-start.2 = (f32[2,16,64,128]{3,2,1,0:T(8,128)S(1)}, f32[2,16,64,128]{3,2,1,0:T(8,128)}, u32[]{:S(2)}) copy-start(f32[2,16,64,128]{3,2,1,0:T(8,128)} %convolution_bitcast_fusion.2) | copy-start | bytes 3145732
  140.5 7.6 %copy-start.3 = (f32[2,16,64,128]{3,2,1,0:T(8,128)S(1)}, f32[2,16,64,128]{3,2,1,0:T(8,128)}, u32[]{:S(2)}) copy-start(f32[2,16,64,128]{3,2,1,0:T(8,128)} %convolution_bitcast_fusion.3) | copy-start | bytes 3145732
  140.5 7.6 %copy-start.4 = (f32[2,16,64,128]{3,2,1,0:T(8,128)S(1)}, f32[2,16,64,128]{3,2,1,0:T(8,128)}, u32[]{:S(2)}) copy-start(f32[2,16,64,128]{3,2,1,0:T(8,128)} %convolution_bitcast_fusion.4) | copy-start | bytes 3145732
  140.5 7.6 %copy-start.5 = (f32[2,16,64,128]{3,2,1,0:T(8,128)S(1)}, f32[2,16,64,128]{3,2,1,0:T(8,128)}, u32[]{:S(2)}) copy-start(f32[2,16,64,128]{3,2,1,0:T(8,128)} %convolution_bitcast_fusion) | copy-start | bytes 3145732
Sparse Core Ops, SparseCore 0:
  107.8 48.5 all-gather.2
